TPU v7x, 256 devices: a whole 4x4x8 slice. The times are simulated.
256 devices in a mesh: feat: 8 (over x, core), rows: 32 (over z, y).
Axes of the slice: x: 4, y: 4, z: 8, core: 2. Of those that a mesh axis runs over, the one named last changes fastest.
Arguments:
- features: bfloat16 [65536, 8192], P('rows', 'feat'), may hold values from -6 to 6
- residual: float32 [65536, 1024], P('rows', 'feat'), may hold values from -8 to 8
- inverse_grams: float32 [8192, 1024], P('feat'), may hold values from -1 to 1, as said below
Outputs:
- increments: bfloat16 [1024, 8192], P(None, 'feat')
- final_residual: float32 [65536, 1024], P('rows', 'feat')
Inputs may be any that keep to these rules, and one draw needn't show every extreme that they name: `inverse_grams`: each block of 1024 rows is a symmetric positive definite matrix.
All inputs are finite; a program needn't handle non-finite values.
Results may differ from a plain program's by a relative error of at most 0.0051.
Values may be sent and summed in bfloat16 or wider, within the bound.
A program may use at most 64 MiB of HBM per device.

v0:
```python
import jax
import jax.numpy as jnp
from jax import lax
from jax.sharding import PartitionSpec as P


def from_behind(value, axis, steps):
    count = lax.axis_size(axis)
    pairs = [(source, (source + steps) % count) for source in range(count)]
    return lax.ppermute(value, axis, pairs)


def on_device(features, residual, inverse_grams):
    block_total = lax.axis_size("feat")
    block_id = lax.axis_index("feat")
    piece_width = residual.shape[1]
    feat_width = features.shape[1]
    contract_rows = (((0,), (0,)), ((), ()))
    contract_cols = (((1,), (1,)), ((), ()))
    start_incr = jnp.zeros((piece_width * block_total, feat_width), jnp.bfloat16)

    def advance(visit, state_pair):
        current, increments = state_pair
        front_index = (block_id - visit) % block_total
        rounded = current.astype(jnp.bfloat16)
        partial_value = lax.dot_general(
            rounded, features, contract_rows, preferred_element_type=jnp.float32
        )
        summed_term = lax.psum(partial_value, "rows")
        update = lax.dot_general(
            summed_term, inverse_grams, contract_cols, precision=lax.Precision.HIGHEST
        ).astype(jnp.bfloat16)
        current = current - lax.dot_general(
            features, update, contract_cols, preferred_element_type=jnp.float32
        )
        increments = lax.dynamic_update_slice_in_dim(
            increments, update, front_index * piece_width, 0
        )
        current = from_behind(current, "feat", 1)
        return (current, increments)

    final_current, increments = lax.fori_loop(0, block_total, advance, (residual, start_incr))
    return (increments, final_current)


def solution(mesh):
    placed = (P("rows", "feat"), P("rows", "feat"), P("feat", None))
    return jax.shard_map(
        on_device,
        mesh=mesh,
        in_specs=placed,
        out_specs=(P(None, "feat"), P("rows", "feat")),
        check_vma=False,
    )
```

profile of v0, /device:TPU:1, one launch (start us, length us, event | category | flops | bytes accessed | tf_op | source)
XLA Modules:
  0.0 1415.4 jit_solution(5744996908963075979)
XLA Ops:
  7.2 1.6 copy.5
  8.7 1.6 broadcast_in_dim.3
  10.3 1396.9 %while.17 = (s32[]{:T(128)}, f32[2048,128]{0,1:T(8,128)S(1)}, bf16[1024,1024]{1,0:T(8,128)(2,1)}, bf16[2048,1024]{1,0:T(8,128)(2,1)}, f32[1024,1024]{1,0:T(8,128...) while((s32[]{:T(128)}, f32[2048,128]{0,1:T(8,128)S(1)}, ...), condition=%wide.region_2.3_spmd, body=%wide.region_0.2_spmd.sunk | while | flops 2685140992 | bytes 41681292 | solution.py:42
  10.3 3.7 fusion.22
  14.1 149.2 %all-reduce.2.cloned.1.call-done = f32[128,1024]{1,0:T(8,128)} async-done(((f32[128,1024]{1,0:T(8,128)}), f32[128,1024]{1,0:T(8,128)}) %all-reduce.2.cloned.1.call-update) | async-done | bytes 524304 | tf_op jit(solution)/shard_map/while/body/eval_jaxpr/psum | solution.py:29
  163.3 7.6 constant_dynamic-update-slice_fusion.2
  170.9 1.5 fusion.23
  172.4 6.3 collective-permute-start
  178.7 11.7 collective-permute-done
  190.4 3.7 fusion.22
  194.2 143.1 %all-reduce.2.cloned.1.call-done = f32[128,1024]{1,0:T(8,128)} async-done(((f32[128,1024]{1,0:T(8,128)}), f32[128,1024]{1,0:T(8,128)}) %all-reduce.2.cloned.1.call-update) | async-done | bytes 524304 | tf_op jit(solution)/shard_map/while/body/eval_jaxpr/psum | solution.py:29
  337.3 7.6 constant_dynamic-update-slice_fusion.2
  344.8 1.5 fusion.23
  346.4 6.3 collective-permute-start
  352.6 11.7 collective-permute-done
  364.4 3.7 fusion.22
  368.1 143.1 %all-reduce.2.cloned.1.call-done = f32[128,1024]{1,0:T(8,128)} async-done(((f32[128,1024]{1,0:T(8,128)}), f32[128,1024]{1,0:T(8,128)}) %all-reduce.2.cloned.1.call-update) | async-done | bytes 524304 | tf_op jit(solution)/shard_map/while/body/eval_jaxpr/psum | solution.py:29
  511.2 7.6 constant_dynamic-update-slice_fusion.2
  520.3 6.3 collective-permute-start
  526.6 11.7 collective-permute-done
  538.3 3.7 fusion.22
  542.1 142.8 %all-reduce.2.cloned.1.call-done = f32[128,1024]{1,0:T(8,128)} async-done(((f32[128,1024]{1,0:T(8,128)}), f32[128,1024]{1,0:T(8,128)}) %all-reduce.2.cloned.1.call-update) | async-done | bytes 524304 | tf_op jit(solution)/shard_map/while/body/eval_jaxpr/psum | solution.py:29
  684.9 7.6 constant_dynamic-update-slice_fusion.2
  692.4 1.5 fusion.23
  694.0 6.3 collective-permute-start
  700.2 11.7 collective-permute-done
  712.0 3.7 fusion.22
  715.7 142.8 %all-reduce.2.cloned.1.call-done = f32[128,1024]{1,0:T(8,128)} async-done(((f32[128,1024]{1,0:T(8,128)}), f32[128,1024]{1,0:T(8,128)}) %all-reduce.2.cloned.1.call-update) | async-done | bytes 524304 | tf_op jit(solution)/shard_map/while/body/eval_jaxpr/psum | solution.py:29
  858.5 7.6 constant_dynamic-update-slice_fusion.2
  866.1 1.5 fusion.23
  867.6 6.2 collective-permute-start
  873.9 11.7 collective-permute-done
  885.6 3.7 fusion.22
  889.4 142.8 %all-reduce.2.cloned.1.call-done = f32[128,1024]{1,0:T(8,128)} async-done(((f32[128,1024]{1,0:T(8,128)}), f32[128,1024]{1,0:T(8,128)}) %all-reduce.2.cloned.1.call-update) | async-done | bytes 524304 | tf_op jit(solution)/shard_map/while/body/eval_jaxpr/psum | solution.py:29
  1032.2 7.6 constant_dynamic-update-slice_fusion.2
  1041.3 6.3 collective-permute-start
  1047.6 11.7 collective-permute-done
  1059.3 3.7 fusion.22
  1063.1 143.1 %all-reduce.2.cloned.1.call-done = f32[128,1024]{1,0:T(8,128)} async-done(((f32[128,1024]{1,0:T(8,128)}), f32[128,1024]{1,0:T(8,128)}) %all-reduce.2.cloned.1.call-update) | async-done | bytes 524304 | tf_op jit(solution)/shard_map/while/body/eval_jaxpr/psum | solution.py:29
  1206.2 7.6 constant_dynamic-update-slice_fusion.2
  1213.7 1.5 fusion.23
  1215.3 6.3 collective-permute-start
  1221.5 11.7 collective-permute-done
  1233.3 3.7 fusion.22
  1237.0 143.1 %all-reduce.2.cloned.1.call-done = f32[128,1024]{1,0:T(8,128)} async-done(((f32[128,1024]{1,0:T(8,128)}), f32[128,1024]{1,0:T(8,128)}) %all-reduce.2.cloned.1.call-update) | async-done | bytes 524304 | tf_op jit(solution)/shard_map/while/body/eval_jaxpr/psum | solution.py:29
  1380.1 7.6 constant_dynamic-update-slice_fusion.2
  1389.3 6.3 collective-permute-start
  1395.5 11.7 collective-permute-done
  (36 shorter events, 6.1 us)
Async XLA Ops:
  10.3 153.0 %all-reduce.2.cloned.1.call-start = ((), (), s32[]{:S(2)}) async-start(), calls=%async_computation | async-start | bytes 1048576 | tf_op jit(solution)/shard_map/while/body/eval_jaxpr/psum | solution.py:29
  163.3 7.6 copy-start
  172.4 18.0 %collective-permute-start = (f32[2048,128]{0,1:T(8,128)S(1)}, f32[2048,128]{0,1:T(8,128)S(1)}, u32[]{:S(2)}, u32[]{:S(2)}) collective-permute-start(f32[2048,128]{0,1:T(8,128)S(1)} %fusion.23), channel_id=1, source_target_pairs={{0,32},{32,64},{64,96},{96,128},{128,160},{160,192},{192,224},{224... | collective-permute-start | bytes 3145736 | tf_op jit(solution)/shard_map/while/body/eval_jaxpr/ppermute | solution.py:10
  190.4 146.8 %all-reduce.2.cloned.1.call-start = ((), (), s32[]{:S(2)}) async-start(), calls=%async_computation | async-start | bytes 1048576 | tf_op jit(solution)/shard_map/while/body/eval_jaxpr/psum | solution.py:29
  337.3 7.6 copy-start
  346.4 18.0 %collective-permute-start = (f32[2048,128]{0,1:T(8,128)S(1)}, f32[2048,128]{0,1:T(8,128)S(1)}, u32[]{:S(2)}, u32[]{:S(2)}) collective-permute-start(f32[2048,128]{0,1:T(8,128)S(1)} %fusion.23), channel_id=1, source_target_pairs={{0,32},{32,64},{64,96},{96,128},{128,160},{160,192},{192,224},{224... | collective-permute-start | bytes 3145736 | tf_op jit(solution)/shard_map/while/body/eval_jaxpr/ppermute | solution.py:10
  364.4 146.8 %all-reduce.2.cloned.1.call-start = ((), (), s32[]{:S(2)}) async-start(), calls=%async_computation | async-start | bytes 1048576 | tf_op jit(solution)/shard_map/while/body/eval_jaxpr/psum | solution.py:29
  511.2 7.6 copy-start
  520.3 18.0 %collective-permute-start = (f32[2048,128]{0,1:T(8,128)S(1)}, f32[2048,128]{0,1:T(8,128)S(1)}, u32[]{:S(2)}, u32[]{:S(2)}) collective-permute-start(f32[2048,128]{0,1:T(8,128)S(1)} %fusion.23), channel_id=1, source_target_pairs={{0,32},{32,64},{64,96},{96,128},{128,160},{160,192},{192,224},{224... | collective-permute-start | bytes 3145736 | tf_op jit(solution)/shard_map/while/body/eval_jaxpr/ppermute | solution.py:10
  538.3 146.5 %all-reduce.2.cloned.1.call-start = ((), (), s32[]{:S(2)}) async-start(), calls=%async_computation | async-start | bytes 1048576 | tf_op jit(solution)/shard_map/while/body/eval_jaxpr/psum | solution.py:29
  684.9 7.6 copy-start
  694.0 18.0 %collective-permute-start = (f32[2048,128]{0,1:T(8,128)S(1)}, f32[2048,128]{0,1:T(8,128)S(1)}, u32[]{:S(2)}, u32[]{:S(2)}) collective-permute-start(f32[2048,128]{0,1:T(8,128)S(1)} %fusion.23), channel_id=1, source_target_pairs={{0,32},{32,64},{64,96},{96,128},{128,160},{160,192},{192,224},{224... | collective-permute-start | bytes 3145736 | tf_op jit(solution)/shard_map/while/body/eval_jaxpr/ppermute | solution.py:10
  712.0 146.5 %all-reduce.2.cloned.1.call-start = ((), (), s32[]{:S(2)}) async-start(), calls=%async_computation | async-start | bytes 1048576 | tf_op jit(solution)/shard_map/while/body/eval_jaxpr/psum | solution.py:29
  858.5 7.6 copy-start
  867.6 18.0 %collective-permute-start = (f32[2048,128]{0,1:T(8,128)S(1)}, f32[2048,128]{0,1:T(8,128)S(1)}, u32[]{:S(2)}, u32[]{:S(2)}) collective-permute-start(f32[2048,128]{0,1:T(8,128)S(1)} %fusion.23), channel_id=1, source_target_pairs={{0,32},{32,64},{64,96},{96,128},{128,160},{160,192},{192,224},{224... | collective-permute-start | bytes 3145736 | tf_op jit(solution)/shard_map/while/body/eval_jaxpr/ppermute | solution.py:10
  885.6 146.5 %all-reduce.2.cloned.1.call-start = ((), (), s32[]{:S(2)}) async-start(), calls=%async_computation | async-start | bytes 1048576 | tf_op jit(solution)/shard_map/while/body/eval_jaxpr/psum | solution.py:29
  1032.2 7.6 copy-start
  1041.3 18.0 %collective-permute-start = (f32[2048,128]{0,1:T(8,128)S(1)}, f32[2048,128]{0,1:T(8,128)S(1)}, u32[]{:S(2)}, u32[]{:S(2)}) collective-permute-start(f32[2048,128]{0,1:T(8,128)S(1)} %fusion.23), channel_id=1, source_target_pairs={{0,32},{32,64},{64,96},{96,128},{128,160},{160,192},{192,224},{224... | collective-permute-start | bytes 3145736 | tf_op jit(solution)/shard_map/while/body/eval_jaxpr/ppermute | solution.py:10
  1059.3 146.8 %all-reduce.2.cloned.1.call-start = ((), (), s32[]{:S(2)}) async-start(), calls=%async_computation | async-start | bytes 1048576 | tf_op jit(solution)/shard_map/while/body/eval_jaxpr/psum | solution.py:29
  1206.2 7.6 copy-start
  1215.3 18.0 %collective-permute-start = (f32[2048,128]{0,1:T(8,128)S(1)}, f32[2048,128]{0,1:T(8,128)S(1)}, u32[]{:S(2)}, u32[]{:S(2)}) collective-permute-start(f32[2048,128]{0,1:T(8,128)S(1)} %fusion.23), channel_id=1, source_target_pairs={{0,32},{32,64},{64,96},{96,128},{128,160},{160,192},{192,224},{224... | collective-permute-start | bytes 3145736 | tf_op jit(solution)/shard_map/while/body/eval_jaxpr/ppermute | solution.py:10
  1233.3 146.8 %all-reduce.2.cloned.1.call-start = ((), (), s32[]{:S(2)}) async-start(), calls=%async_computation | async-start | bytes 1048576 | tf_op jit(solution)/shard_map/while/body/eval_jaxpr/psum | solution.py:29
  1380.1 7.6 copy-start
  1389.3 18.0 %collective-permute-start = (f32[2048,128]{0,1:T(8,128)S(1)}, f32[2048,128]{0,1:T(8,128)S(1)}, u32[]{:S(2)}, u32[]{:S(2)}) collective-permute-start(f32[2048,128]{0,1:T(8,128)S(1)} %fusion.23), channel_id=1, source_target_pairs={{0,32},{32,64},{64,96},{96,128},{128,160},{160,192},{192,224},{224... | collective-permute-start | bytes 3145736 | tf_op jit(solution)/shard_map/while/body/eval_jaxpr/ppermute | solution.py:10
Sparse Core Ops, SparseCore 0:
  15.1 148.1 all-reduce.1
  195.2 142.0 all-reduce.1
  369.2 141.9 all-reduce.1
  542.8 142.0 all-reduce.1
  716.4 142.0 all-reduce.1
  890.1 142.0 all-reduce.1
  1064.1 142.0 all-reduce.1
  1238.1 142.0 all-reduce.1
where the time goes:
time: 1420 us
  waiting for transfers between devices  1240 us (87%)
  matrix products  102 us (7%)
  starting transfers between devices  50.1 us (4%)
    psum x8, waiting for transfers between devices, advance(): summed_term = lax.psum(partial_value, 'rows')  1150 us
    ppermute x8, waiting for transfers between devices, from_behind(): return lax.ppermute(value, axis, pairs)  93.9 us
    dot_general x8, matrix products, advance(): lax.dot_general(summed_term, inverse_grams, contract_cols, precision=lax....  60.7 us
    ppermute x8, starting transfers between devices, from_behind(): return lax.ppermute(value, axis, pairs)  50.1 us
    dot_general x8, matrix products, advance(): lax.dot_general(rounded, features, contract_rows, preferred_element_type=...  29.6 us
  transfers between devices with their start and end apart: 16, of which 16 were waited for; matrix products, arithmetic and copies ran while one was open for 0% of the time, Pallas kernels for 0%

commit v1 on v0

--- a/solution.py
+++ b/solution.py
@@ -26,7 +26,10 @@
         partial_value = lax.dot_general(
             rounded, features, contract_rows, preferred_element_type=jnp.float32
         )
-        summed_term = lax.psum(partial_value, "rows")
+        size, summed_term = (lax.axis_size("rows"), partial_value)
+        for stride in [1 << k for k in range(size.bit_length() - 1)]:
+            route = [(i, i ^ stride) for i in range(size)]
+            summed_term = summed_term + lax.ppermute(summed_term, "rows", route)
         update = lax.dot_general(
             summed_term, inverse_grams, contract_cols, precision=lax.Precision.HIGHEST
         ).astype(jnp.bfloat16)

time: 1420 us -> 960 us (0.68)
  waiting for transfers between devices: 1240 us -> 691 us
  starting transfers between devices: 50.1 us -> 154 us
    psum x8 -> x0, waiting for transfers between devices: 1150 us -> none  [advance(): summed_term = lax.psum(partial_value, 'rows')]
    ppermute x0 -> x40, waiting for transfers between devices: none -> 597 us  [advance(): summed_term = summed_term + lax.ppermute(summed_term, 'rows', route)]
    ppermute x0 -> x40, starting transfers between devices: none -> 77.9 us  [advance(): summed_term = summed_term + lax.ppermute(summed_term, 'rows', route)]
    ppermute x8, starting transfers between devices: 50.1 us -> 75.7 us  [from_behind(): return lax.ppermute(value, axis, pairs)]
  transfers between devices with their start and end apart: 16 -> 48, of which waited for: 16 -> 48; matrix products, arithmetic and copies ran while one was open for 0% -> 0% of each run, Pallas kernels for 0% -> 0%
where the time goes in v1:
time: 960 us; the launch traced here: 945 us
  waiting for transfers between devices  691 us (72%)
  starting transfers between devices  154 us (16%)
  matrix products  93.2 us (10%)
    ppermute x40, waiting for transfers between devices, advance(): summed_term = summed_term + lax.ppermute(summed_term, 'rows', route)  597 us
    ppermute x8, waiting for transfers between devices, from_behind(): return lax.ppermute(value, axis, pairs)  93.9 us
    ppermute x40, starting transfers between devices, advance(): summed_term = summed_term + lax.ppermute(summed_term, 'rows', route)  77.9 us
    ppermute x8, starting transfers between devices, from_behind(): return lax.ppermute(value, axis, pairs)  75.7 us
    dot_general x8, matrix products, advance(): lax.dot_general(summed_term, inverse_grams, contract_cols, precision=lax....  57.8 us
    dot_general x8, matrix products, advance(): lax.dot_general(rounded, features, contract_rows, preferred_element_type=...  23.2 us
  transfers between devices with their start and end apart: 48, of which 48 were waited for; matrix products, arithmetic and copies ran while one was open for 0% of the time, Pallas kernels for 0%

profile of v1, /device:TPU:1, one launch (start us, length us, event | category | flops | bytes accessed | tf_op | source)
XLA Modules:
  0.0 945.0 jit_solution(1106211221373536959)
XLA Ops:
  3.8 940.0 %while.17 = (s32[]{:T(128)}, f32[2048,128]{0,1:T(8,128)S(1)}, bf16[1024,1024]{1,0:T(8,128)(2,1)}, bf16[2048,1024]{1,0:T(8,128)(2,1)}, f32[1024,1024]{1,0:T(8,128...) while((s32[]{:T(128)}, f32[2048,128]{0,1:T(8,128)S(1)}, ...), condition=%wide.region_1.2_spmd, body=%wide.region_0.1_spmd.sunk | while | flops 2685665280 | bytes 55837228 | solution.py:45
  8.9 10.5 %collective-permute-done = f32[128,1024]{1,0:T(8,128)S(1)} collective-permute-done((f32[128,1024]{1,0:T(8,128)S(1)}, f32[128,1024]{1,0:T(8,128)S(1)}, u32[]{:S(2)}, u32[]{:S(2)}) %collective-permute-start) | collective-permute-done | bytes 524320 | tf_op jit(solution)/shard_map/while/body/eval_jaxpr/ppermute | solution.py:32
  23.5 10.6 %collective-permute-done.1 = f32[128,1024]{1,0:T(8,128)S(1)} collective-permute-done((f32[128,1024]{1,0:T(8,128)S(1)}, f32[128,1024]{1,0:T(8,128)S(1)}, u32[]{:S(2)}, u32[]{:S(2)}) %collective-permute-start.1) | collective-permute-done | bytes 524320 | tf_op jit(solution)/shard_map/while/body/eval_jaxpr/ppermute | solution.py:32
  35.8 9.9 %collective-permute-done.2 = f32[128,1024]{1,0:T(8,128)S(1)} collective-permute-done((f32[128,1024]{1,0:T(8,128)S(1)}, f32[128,1024]{1,0:T(8,128)S(1)}, u32[]{:S(2)}, u32[]{:S(2)}) %collective-permute-start.2) | collective-permute-done | bytes 524320 | tf_op jit(solution)/shard_map/while/body/eval_jaxpr/ppermute | solution.py:32
  48.8 22.6 %collective-permute-done.3 = f32[128,1024]{1,0:T(8,128)S(1)} collective-permute-done((f32[128,1024]{1,0:T(8,128)S(1)}, f32[128,1024]{1,0:T(8,128)S(1)}, u32[]{:S(2)}, u32[]{:S(2)}) %collective-permute-start.3) | collective-permute-done | bytes 524320 | tf_op jit(solution)/shard_map/while/body/eval_jaxpr/ppermute | solution.py:32
  78.0 22.7 %collective-permute-done.4 = f32[128,1024]{1,0:T(8,128)S(1)} collective-permute-done((f32[128,1024]{1,0:T(8,128)S(1)}, f32[128,1024]{1,0:T(8,128)S(1)}, u32[]{:S(2)}, u32[]{:S(2)}) %collective-permute-start.4) | collective-permute-done | bytes 524320 | tf_op jit(solution)/shard_map/while/body/eval_jaxpr/ppermute | solution.py:32
  112.1 11.7 %collective-permute-done.5 = f32[2048,128]{0,1:T(8,128)S(1)} collective-permute-done((f32[2048,128]{0,1:T(8,128)S(1)}, f32[2048,128]{0,1:T(8,128)S(1)}, u32[]{:S(2)}, u32[]{:S(2)}) %collective-permute-start.5) | collective-permute-done | bytes 1048608 | tf_op jit(solution)/shard_map/while/body/eval_jaxpr/ppermute | solution.py:10
  128.2 9.6 %collective-permute-done = f32[128,1024]{1,0:T(8,128)S(1)} collective-permute-done((f32[128,1024]{1,0:T(8,128)S(1)}, f32[128,1024]{1,0:T(8,128)S(1)}, u32[]{:S(2)}, u32[]{:S(2)}) %collective-permute-start) | collective-permute-done | bytes 524320 | tf_op jit(solution)/shard_map/while/body/eval_jaxpr/ppermute | solution.py:32
  140.8 10.9 %collective-permute-done.1 = f32[128,1024]{1,0:T(8,128)S(1)} collective-permute-done((f32[128,1024]{1,0:T(8,128)S(1)}, f32[128,1024]{1,0:T(8,128)S(1)}, u32[]{:S(2)}, u32[]{:S(2)}) %collective-permute-start.1) | collective-permute-done | bytes 524320 | tf_op jit(solution)/shard_map/while/body/eval_jaxpr/ppermute | solution.py:32
  151.9 10.3 %collective-permute-done.2 = f32[128,1024]{1,0:T(8,128)S(1)} collective-permute-done((f32[128,1024]{1,0:T(8,128)S(1)}, f32[128,1024]{1,0:T(8,128)S(1)}, u32[]{:S(2)}, u32[]{:S(2)}) %collective-permute-start.2) | collective-permute-done | bytes 524320 | tf_op jit(solution)/shard_map/while/body/eval_jaxpr/ppermute | solution.py:32
  164.6 22.2 %collective-permute-done.3 = f32[128,1024]{1,0:T(8,128)S(1)} collective-permute-done((f32[128,1024]{1,0:T(8,128)S(1)}, f32[128,1024]{1,0:T(8,128)S(1)}, u32[]{:S(2)}, u32[]{:S(2)}) %collective-permute-start.3) | collective-permute-done | bytes 524320 | tf_op jit(solution)/shard_map/while/body/eval_jaxpr/ppermute | solution.py:32
  190.5 25.0 %collective-permute-done.4 = f32[128,1024]{1,0:T(8,128)S(1)} collective-permute-done((f32[128,1024]{1,0:T(8,128)S(1)}, f32[128,1024]{1,0:T(8,128)S(1)}, u32[]{:S(2)}, u32[]{:S(2)}) %collective-permute-start.4) | collective-permute-done | bytes 524320 | tf_op jit(solution)/shard_map/while/body/eval_jaxpr/ppermute | solution.py:32
  227.0 11.7 %collective-permute-done.5 = f32[2048,128]{0,1:T(8,128)S(1)} collective-permute-done((f32[2048,128]{0,1:T(8,128)S(1)}, f32[2048,128]{0,1:T(8,128)S(1)}, u32[]{:S(2)}, u32[]{:S(2)}) %collective-permute-start.5) | collective-permute-done | bytes 1048608 | tf_op jit(solution)/shard_map/while/body/eval_jaxpr/ppermute | solution.py:10
  242.9 10.8 %collective-permute-done = f32[128,1024]{1,0:T(8,128)S(1)} collective-permute-done((f32[128,1024]{1,0:T(8,128)S(1)}, f32[128,1024]{1,0:T(8,128)S(1)}, u32[]{:S(2)}, u32[]{:S(2)}) %collective-permute-start) | collective-permute-done | bytes 524320 | tf_op jit(solution)/shard_map/while/body/eval_jaxpr/ppermute | solution.py:32
  256.2 11.5 %collective-permute-done.1 = f32[128,1024]{1,0:T(8,128)S(1)} collective-permute-done((f32[128,1024]{1,0:T(8,128)S(1)}, f32[128,1024]{1,0:T(8,128)S(1)}, u32[]{:S(2)}, u32[]{:S(2)}) %collective-permute-start.1) | collective-permute-done | bytes 524320 | tf_op jit(solution)/shard_map/while/body/eval_jaxpr/ppermute | solution.py:32
  267.8 11.4 %collective-permute-done.2 = f32[128,1024]{1,0:T(8,128)S(1)} collective-permute-done((f32[128,1024]{1,0:T(8,128)S(1)}, f32[128,1024]{1,0:T(8,128)S(1)}, u32[]{:S(2)}, u32[]{:S(2)}) %collective-permute-start.2) | collective-permute-done | bytes 524320 | tf_op jit(solution)/shard_map/while/body/eval_jaxpr/ppermute | solution.py:32
  283.6 22.7 %collective-permute-done.3 = f32[128,1024]{1,0:T(8,128)S(1)} collective-permute-done((f32[128,1024]{1,0:T(8,128)S(1)}, f32[128,1024]{1,0:T(8,128)S(1)}, u32[]{:S(2)}, u32[]{:S(2)}) %collective-permute-start.3) | collective-permute-done | bytes 524320 | tf_op jit(solution)/shard_map/while/body/eval_jaxpr/ppermute | solution.py:32
  309.5 25.9 %collective-permute-done.4 = f32[128,1024]{1,0:T(8,128)S(1)} collective-permute-done((f32[128,1024]{1,0:T(8,128)S(1)}, f32[128,1024]{1,0:T(8,128)S(1)}, u32[]{:S(2)}, u32[]{:S(2)}) %collective-permute-start.4) | collective-permute-done | bytes 524320 | tf_op jit(solution)/shard_map/while/body/eval_jaxpr/ppermute | solution.py:32
  344.2 11.7 %collective-permute-done.5 = f32[2048,128]{0,1:T(8,128)S(1)} collective-permute-done((f32[2048,128]{0,1:T(8,128)S(1)}, f32[2048,128]{0,1:T(8,128)S(1)}, u32[]{:S(2)}, u32[]{:S(2)}) %collective-permute-start.5) | collective-permute-done | bytes 1048608 | tf_op jit(solution)/shard_map/while/body/eval_jaxpr/ppermute | solution.py:10
  358.9 9.3 collective-permute-done
  372.8 8.3 collective-permute-done.1
  392.5 11.1 %collective-permute-done.3 = f32[128,1024]{1,0:T(8,128)S(1)} collective-permute-done((f32[128,1024]{1,0:T(8,128)S(1)}, f32[128,1024]{1,0:T(8,128)S(1)}, u32[]{:S(2)}, u32[]{:S(2)}) %collective-permute-start.3) | collective-permute-done | bytes 524320 | tf_op jit(solution)/shard_map/while/body/eval_jaxpr/ppermute | solution.py:32
  406.1 19.7 %collective-permute-done.4 = f32[128,1024]{1,0:T(8,128)S(1)} collective-permute-done((f32[128,1024]{1,0:T(8,128)S(1)}, f32[128,1024]{1,0:T(8,128)S(1)}, u32[]{:S(2)}, u32[]{:S(2)}) %collective-permute-start.4) | collective-permute-done | bytes 524320 | tf_op jit(solution)/shard_map/while/body/eval_jaxpr/ppermute | solution.py:32
  434.6 19.7 %collective-permute-start.5 = (f32[2048,128]{0,1:T(8,128)S(1)}, f32[2048,128]{0,1:T(8,128)S(1)}, u32[]{:S(2)}, u32[]{:S(2)}) collective-permute-start(f32[2048,128]{0,1:T(8,128)S(1)} %fusion.21), channel_id=1, source_target_pairs={{0,32},{32,64},{64,96},{96,128},{128,160},{160,192},{192,224},{224... | collective-permute-start | bytes 3145736 | tf_op jit(solution)/shard_map/while/body/eval_jaxpr/ppermute | solution.py:10
  454.3 11.7 %collective-permute-done.5 = f32[2048,128]{0,1:T(8,128)S(1)} collective-permute-done((f32[2048,128]{0,1:T(8,128)S(1)}, f32[2048,128]{0,1:T(8,128)S(1)}, u32[]{:S(2)}, u32[]{:S(2)}) %collective-permute-start.5) | collective-permute-done | bytes 1048608 | tf_op jit(solution)/shard_map/while/body/eval_jaxpr/ppermute | solution.py:10
  469.1 8.0 collective-permute-done
  479.0 12.5 %collective-permute-done.1 = f32[128,1024]{1,0:T(8,128)S(1)} collective-permute-done((f32[128,1024]{1,0:T(8,128)S(1)}, f32[128,1024]{1,0:T(8,128)S(1)}, u32[]{:S(2)}, u32[]{:S(2)}) %collective-permute-start.1) | collective-permute-done | bytes 524320 | tf_op jit(solution)/shard_map/while/body/eval_jaxpr/ppermute | solution.py:32
  491.7 8.3 collective-permute-done.2
  502.2 12.6 %collective-permute-done.3 = f32[128,1024]{1,0:T(8,128)S(1)} collective-permute-done((f32[128,1024]{1,0:T(8,128)S(1)}, f32[128,1024]{1,0:T(8,128)S(1)}, u32[]{:S(2)}, u32[]{:S(2)}) %collective-permute-start.3) | collective-permute-done | bytes 524320 | tf_op jit(solution)/shard_map/while/body/eval_jaxpr/ppermute | solution.py:32
  517.7 19.5 %collective-permute-done.4 = f32[128,1024]{1,0:T(8,128)S(1)} collective-permute-done((f32[128,1024]{1,0:T(8,128)S(1)}, f32[128,1024]{1,0:T(8,128)S(1)}, u32[]{:S(2)}, u32[]{:S(2)}) %collective-permute-start.4) | collective-permute-done | bytes 524320 | tf_op jit(solution)/shard_map/while/body/eval_jaxpr/ppermute | solution.py:32
  546.0 29.5 %collective-permute-start.5 = (f32[2048,128]{0,1:T(8,128)S(1)}, f32[2048,128]{0,1:T(8,128)S(1)}, u32[]{:S(2)}, u32[]{:S(2)}) collective-permute-start(f32[2048,128]{0,1:T(8,128)S(1)} %fusion.21), channel_id=1, source_target_pairs={{0,32},{32,64},{64,96},{96,128},{128,160},{160,192},{192,224},{224... | collective-permute-start | bytes 3145736 | tf_op jit(solution)/shard_map/while/body/eval_jaxpr/ppermute | solution.py:10
  575.5 11.7 %collective-permute-done.5 = f32[2048,128]{0,1:T(8,128)S(1)} collective-permute-done((f32[2048,128]{0,1:T(8,128)S(1)}, f32[2048,128]{0,1:T(8,128)S(1)}, u32[]{:S(2)}, u32[]{:S(2)}) %collective-permute-start.5) | collective-permute-done | bytes 1048608 | tf_op jit(solution)/shard_map/while/body/eval_jaxpr/ppermute | solution.py:10
  591.5 12.7 %collective-permute-done = f32[128,1024]{1,0:T(8,128)S(1)} collective-permute-done((f32[128,1024]{1,0:T(8,128)S(1)}, f32[128,1024]{1,0:T(8,128)S(1)}, u32[]{:S(2)}, u32[]{:S(2)}) %collective-permute-start) | collective-permute-done | bytes 524320 | tf_op jit(solution)/shard_map/while/body/eval_jaxpr/ppermute | solution.py:32
  604.3 14.6 %collective-permute-done.1 = f32[128,1024]{1,0:T(8,128)S(1)} collective-permute-done((f32[128,1024]{1,0:T(8,128)S(1)}, f32[128,1024]{1,0:T(8,128)S(1)}, u32[]{:S(2)}, u32[]{:S(2)}) %collective-permute-start.1) | collective-permute-done | bytes 524320 | tf_op jit(solution)/shard_map/while/body/eval_jaxpr/ppermute | solution.py:32
  619.1 12.2 %collective-permute-done.2 = f32[128,1024]{1,0:T(8,128)S(1)} collective-permute-done((f32[128,1024]{1,0:T(8,128)S(1)}, f32[128,1024]{1,0:T(8,128)S(1)}, u32[]{:S(2)}, u32[]{:S(2)}) %collective-permute-start.2) | collective-permute-done | bytes 524320 | tf_op jit(solution)/shard_map/while/body/eval_jaxpr/ppermute | solution.py:32
  633.5 23.4 %collective-permute-done.3 = f32[128,1024]{1,0:T(8,128)S(1)} collective-permute-done((f32[128,1024]{1,0:T(8,128)S(1)}, f32[128,1024]{1,0:T(8,128)S(1)}, u32[]{:S(2)}, u32[]{:S(2)}) %collective-permute-start.3) | collective-permute-done | bytes 524320 | tf_op jit(solution)/shard_map/while/body/eval_jaxpr/ppermute | solution.py:32
  659.9 25.9 %collective-permute-done.4 = f32[128,1024]{1,0:T(8,128)S(1)} collective-permute-done((f32[128,1024]{1,0:T(8,128)S(1)}, f32[128,1024]{1,0:T(8,128)S(1)}, u32[]{:S(2)}, u32[]{:S(2)}) %collective-permute-start.4) | collective-permute-done | bytes 524320 | tf_op jit(solution)/shard_map/while/body/eval_jaxpr/ppermute | solution.py:32
  694.5 11.7 %collective-permute-done.5 = f32[2048,128]{0,1:T(8,128)S(1)} collective-permute-done((f32[2048,128]{0,1:T(8,128)S(1)}, f32[2048,128]{0,1:T(8,128)S(1)}, u32[]{:S(2)}, u32[]{:S(2)}) %collective-permute-start.5) | collective-permute-done | bytes 1048608 | tf_op jit(solution)/shard_map/while/body/eval_jaxpr/ppermute | solution.py:10
  725.4 9.0 collective-permute-done.1
  734.6 9.6 %collective-permute-done.2 = f32[128,1024]{1,0:T(8,128)S(1)} collective-permute-done((f32[128,1024]{1,0:T(8,128)S(1)}, f32[128,1024]{1,0:T(8,128)S(1)}, u32[]{:S(2)}, u32[]{:S(2)}) %collective-permute-start.2) | collective-permute-done | bytes 524320 | tf_op jit(solution)/shard_map/while/body/eval_jaxpr/ppermute | solution.py:32
  744.4 48.6 %collective-permute-done.3 = f32[128,1024]{1,0:T(8,128)S(1)} collective-permute-done((f32[128,1024]{1,0:T(8,128)S(1)}, f32[128,1024]{1,0:T(8,128)S(1)}, u32[]{:S(2)}, u32[]{:S(2)}) %collective-permute-start.3) | collective-permute-done | bytes 524320 | tf_op jit(solution)/shard_map/while/body/eval_jaxpr/ppermute | solution.py:32
  793.2 25.3 %collective-permute-done.4 = f32[128,1024]{1,0:T(8,128)S(1)} collective-permute-done((f32[128,1024]{1,0:T(8,128)S(1)}, f32[128,1024]{1,0:T(8,128)S(1)}, u32[]{:S(2)}, u32[]{:S(2)}) %collective-permute-start.4) | collective-permute-done | bytes 524320 | tf_op jit(solution)/shard_map/while/body/eval_jaxpr/ppermute | solution.py:32
  827.3 11.7 %collective-permute-done.5 = f32[2048,128]{0,1:T(8,128)S(1)} collective-permute-done((f32[2048,128]{0,1:T(8,128)S(1)}, f32[2048,128]{0,1:T(8,128)S(1)}, u32[]{:S(2)}, u32[]{:S(2)}) %collective-permute-start.5) | collective-permute-done | bytes 1048608 | tf_op jit(solution)/shard_map/while/body/eval_jaxpr/ppermute | solution.py:10
  852.6 9.6 %collective-permute-done.1 = f32[128,1024]{1,0:T(8,128)S(1)} collective-permute-done((f32[128,1024]{1,0:T(8,128)S(1)}, f32[128,1024]{1,0:T(8,128)S(1)}, u32[]{:S(2)}, u32[]{:S(2)}) %collective-permute-start.1) | collective-permute-done | bytes 524320 | tf_op jit(solution)/shard_map/while/body/eval_jaxpr/ppermute | solution.py:32
  870.6 14.9 %collective-permute-done.3 = f32[128,1024]{1,0:T(8,128)S(1)} collective-permute-done((f32[128,1024]{1,0:T(8,128)S(1)}, f32[128,1024]{1,0:T(8,128)S(1)}, u32[]{:S(2)}, u32[]{:S(2)}) %collective-permute-start.3) | collective-permute-done | bytes 524320 | tf_op jit(solution)/shard_map/while/body/eval_jaxpr/ppermute | solution.py:32
  889.2 13.0 %collective-permute-done.4 = f32[128,1024]{1,0:T(8,128)S(1)} collective-permute-done((f32[128,1024]{1,0:T(8,128)S(1)}, f32[128,1024]{1,0:T(8,128)S(1)}, u32[]{:S(2)}, u32[]{:S(2)}) %collective-permute-start.4) | collective-permute-done | bytes 524320 | tf_op jit(solution)/shard_map/while/body/eval_jaxpr/ppermute | solution.py:32
  911.0 21.0 %collective-permute-start.5 = (f32[2048,128]{0,1:T(8,128)S(1)}, f32[2048,128]{0,1:T(8,128)S(1)}, u32[]{:S(2)}, u32[]{:S(2)}) collective-permute-start(f32[2048,128]{0,1:T(8,128)S(1)} %fusion.21), channel_id=1, source_target_pairs={{0,32},{32,64},{64,96},{96,128},{128,160},{160,192},{192,224},{224... | collective-permute-start | bytes 3145736 | tf_op jit(solution)/shard_map/while/body/eval_jaxpr/ppermute | solution.py:10
  932.0 11.7 %collective-permute-done.5 = f32[2048,128]{0,1:T(8,128)S(1)} collective-permute-done((f32[2048,128]{0,1:T(8,128)S(1)}, f32[2048,128]{0,1:T(8,128)S(1)}, u32[]{:S(2)}, u32[]{:S(2)}) %collective-permute-start.5) | collective-permute-done | bytes 1048608 | tf_op jit(solution)/shard_map/while/body/eval_jaxpr/ppermute | solution.py:10
  (124 shorter events, 215.0 us)
Async XLA Ops:
  6.7 12.7 %collective-permute-start = (f32[128,1024]{1,0:T(8,128)S(1)}, f32[128,1024]{1,0:T(8,128)S(1)}, u32[]{:S(2)}, u32[]{:S(2)}) collective-permute-start(f32[128,1024]{1,0:T(8,128)S(1)} %fusion.20), channel_id=1, source_target_pairs={{0,1},{1,0},{2,3},{3,2},{4,5},{5,4},{6,7},{7,6},{8,9},{9,8},{10,11... | collective-permute-start | bytes 1572872 | tf_op jit(solution)/shard_map/while/body/eval_jaxpr/ppermute | solution.py:32
  19.4 14.6 %collective-permute-start.1 = (f32[128,1024]{1,0:T(8,128)S(1)}, f32[128,1024]{1,0:T(8,128)S(1)}, u32[]{:S(2)}, u32[]{:S(2)}) collective-permute-start(f32[128,1024]{1,0:T(8,128)S(1)} %add.107), channel_id=1, source_target_pairs={{0,2},{1,3},{2,0},{3,1},{4,6},{5,7},{6,4},{7,5},{8,10},{9,11},{10,... | collective-permute-start | bytes 1572872 | tf_op jit(solution)/shard_map/while/body/eval_jaxpr/ppermute | solution.py:32
  34.1 11.5 %collective-permute-start.2 = (f32[128,1024]{1,0:T(8,128)S(1)}, f32[128,1024]{1,0:T(8,128)S(1)}, u32[]{:S(2)}, u32[]{:S(2)}) collective-permute-start(f32[128,1024]{1,0:T(8,128)S(1)} %add.108), channel_id=1, source_target_pairs={{0,4},{1,5},{2,6},{3,7},{4,0},{5,1},{6,2},{7,3},{8,12},{9,13},{10,... | collective-permute-start | bytes 1572872 | tf_op jit(solution)/shard_map/while/body/eval_jaxpr/ppermute | solution.py:32
  45.7 25.7 %collective-permute-start.3 = (f32[128,1024]{1,0:T(8,128)S(1)}, f32[128,1024]{1,0:T(8,128)S(1)}, u32[]{:S(2)}, u32[]{:S(2)}) collective-permute-start(f32[128,1024]{1,0:T(8,128)S(1)} %add.109), channel_id=1, source_target_pairs={{0,8},{1,9},{2,10},{3,11},{4,12},{5,13},{6,14},{7,15},{8,0},{9,1},... | collective-permute-start | bytes 1572872 | tf_op jit(solution)/shard_map/while/body/eval_jaxpr/ppermute | solution.py:32
  71.5 29.2 %collective-permute-start.4 = (f32[128,1024]{1,0:T(8,128)S(1)}, f32[128,1024]{1,0:T(8,128)S(1)}, u32[]{:S(2)}, u32[]{:S(2)}) collective-permute-start(f32[128,1024]{1,0:T(8,128)S(1)} %add.110), channel_id=1, source_target_pairs={{0,16},{1,17},{2,18},{3,19},{4,20},{5,21},{6,22},{7,23},{8,24},{9,... | collective-permute-start | bytes 1572872 | tf_op jit(solution)/shard_map/while/body/eval_jaxpr/ppermute | solution.py:32
  109.4 14.4 %collective-permute-start.5 = (f32[2048,128]{0,1:T(8,128)S(1)}, f32[2048,128]{0,1:T(8,128)S(1)}, u32[]{:S(2)}, u32[]{:S(2)}) collective-permute-start(f32[2048,128]{0,1:T(8,128)S(1)} %fusion.21), channel_id=1, source_target_pairs={{0,32},{32,64},{64,96},{96,128},{128,160},{160,192},{192,224},{224... | collective-permute-start | bytes 3145736 | tf_op jit(solution)/shard_map/while/body/eval_jaxpr/ppermute | solution.py:10
  126.8 11.0 %collective-permute-start = (f32[128,1024]{1,0:T(8,128)S(1)}, f32[128,1024]{1,0:T(8,128)S(1)}, u32[]{:S(2)}, u32[]{:S(2)}) collective-permute-start(f32[128,1024]{1,0:T(8,128)S(1)} %fusion.20), channel_id=1, source_target_pairs={{0,1},{1,0},{2,3},{3,2},{4,5},{5,4},{6,7},{7,6},{8,9},{9,8},{10,11... | collective-permute-start | bytes 1572872 | tf_op jit(solution)/shard_map/while/body/eval_jaxpr/ppermute | solution.py:32
  137.8 13.9 %collective-permute-start.1 = (f32[128,1024]{1,0:T(8,128)S(1)}, f32[128,1024]{1,0:T(8,128)S(1)}, u32[]{:S(2)}, u32[]{:S(2)}) collective-permute-start(f32[128,1024]{1,0:T(8,128)S(1)} %add.107), channel_id=1, source_target_pairs={{0,2},{1,3},{2,0},{3,1},{4,6},{5,7},{6,4},{7,5},{8,10},{9,11},{10,... | collective-permute-start | bytes 1572872 | tf_op jit(solution)/shard_map/while/body/eval_jaxpr/ppermute | solution.py:32
  151.8 10.4 %collective-permute-start.2 = (f32[128,1024]{1,0:T(8,128)S(1)}, f32[128,1024]{1,0:T(8,128)S(1)}, u32[]{:S(2)}, u32[]{:S(2)}) collective-permute-start(f32[128,1024]{1,0:T(8,128)S(1)} %add.108), channel_id=1, source_target_pairs={{0,4},{1,5},{2,6},{3,7},{4,0},{5,1},{6,2},{7,3},{8,12},{9,13},{10,... | collective-permute-start | bytes 1572872 | tf_op jit(solution)/shard_map/while/body/eval_jaxpr/ppermute | solution.py:32
  162.2 24.6 %collective-permute-start.3 = (f32[128,1024]{1,0:T(8,128)S(1)}, f32[128,1024]{1,0:T(8,128)S(1)}, u32[]{:S(2)}, u32[]{:S(2)}) collective-permute-start(f32[128,1024]{1,0:T(8,128)S(1)} %add.109), channel_id=1, source_target_pairs={{0,8},{1,9},{2,10},{3,11},{4,12},{5,13},{6,14},{7,15},{8,0},{9,1},... | collective-permute-start | bytes 1572872 | tf_op jit(solution)/shard_map/while/body/eval_jaxpr/ppermute | solution.py:32
  186.9 28.6 %collective-permute-start.4 = (f32[128,1024]{1,0:T(8,128)S(1)}, f32[128,1024]{1,0:T(8,128)S(1)}, u32[]{:S(2)}, u32[]{:S(2)}) collective-permute-start(f32[128,1024]{1,0:T(8,128)S(1)} %add.110), channel_id=1, source_target_pairs={{0,16},{1,17},{2,18},{3,19},{4,20},{5,21},{6,22},{7,23},{8,24},{9,... | collective-permute-start | bytes 1572872 | tf_op jit(solution)/shard_map/while/body/eval_jaxpr/ppermute | solution.py:32
  224.3 14.5 %collective-permute-start.5 = (f32[2048,128]{0,1:T(8,128)S(1)}, f32[2048,128]{0,1:T(8,128)S(1)}, u32[]{:S(2)}, u32[]{:S(2)}) collective-permute-start(f32[2048,128]{0,1:T(8,128)S(1)} %fusion.21), channel_id=1, source_target_pairs={{0,32},{32,64},{64,96},{96,128},{128,160},{160,192},{192,224},{224... | collective-permute-start | bytes 3145736 | tf_op jit(solution)/shard_map/while/body/eval_jaxpr/ppermute | solution.py:10
  241.7 12.0 %collective-permute-start = (f32[128,1024]{1,0:T(8,128)S(1)}, f32[128,1024]{1,0:T(8,128)S(1)}, u32[]{:S(2)}, u32[]{:S(2)}) collective-permute-start(f32[128,1024]{1,0:T(8,128)S(1)} %fusion.20), channel_id=1, source_target_pairs={{0,1},{1,0},{2,3},{3,2},{4,5},{5,4},{6,7},{7,6},{8,9},{9,8},{10,11... | collective-permute-start | bytes 1572872 | tf_op jit(solution)/shard_map/while/body/eval_jaxpr/ppermute | solution.py:32
  253.8 13.9 %collective-permute-start.1 = (f32[128,1024]{1,0:T(8,128)S(1)}, f32[128,1024]{1,0:T(8,128)S(1)}, u32[]{:S(2)}, u32[]{:S(2)}) collective-permute-start(f32[128,1024]{1,0:T(8,128)S(1)} %add.107), channel_id=1, source_target_pairs={{0,2},{1,3},{2,0},{3,1},{4,6},{5,7},{6,4},{7,5},{8,10},{9,11},{10,... | collective-permute-start | bytes 1572872 | tf_op jit(solution)/shard_map/while/body/eval_jaxpr/ppermute | solution.py:32
  267.7 11.5 %collective-permute-start.2 = (f32[128,1024]{1,0:T(8,128)S(1)}, f32[128,1024]{1,0:T(8,128)S(1)}, u32[]{:S(2)}, u32[]{:S(2)}) collective-permute-start(f32[128,1024]{1,0:T(8,128)S(1)} %add.108), channel_id=1, source_target_pairs={{0,4},{1,5},{2,6},{3,7},{4,0},{5,1},{6,2},{7,3},{8,12},{9,13},{10,... | collective-permute-start | bytes 1572872 | tf_op jit(solution)/shard_map/while/body/eval_jaxpr/ppermute | solution.py:32
  279.3 27.1 %collective-permute-start.3 = (f32[128,1024]{1,0:T(8,128)S(1)}, f32[128,1024]{1,0:T(8,128)S(1)}, u32[]{:S(2)}, u32[]{:S(2)}) collective-permute-start(f32[128,1024]{1,0:T(8,128)S(1)} %add.109), channel_id=1, source_target_pairs={{0,8},{1,9},{2,10},{3,11},{4,12},{5,13},{6,14},{7,15},{8,0},{9,1},... | collective-permute-start | bytes 1572872 | tf_op jit(solution)/shard_map/while/body/eval_jaxpr/ppermute | solution.py:32
  306.4 29.0 %collective-permute-start.4 = (f32[128,1024]{1,0:T(8,128)S(1)}, f32[128,1024]{1,0:T(8,128)S(1)}, u32[]{:S(2)}, u32[]{:S(2)}) collective-permute-start(f32[128,1024]{1,0:T(8,128)S(1)} %add.110), channel_id=1, source_target_pairs={{0,16},{1,17},{2,18},{3,19},{4,20},{5,21},{6,22},{7,23},{8,24},{9,... | collective-permute-start | bytes 1572872 | tf_op jit(solution)/shard_map/while/body/eval_jaxpr/ppermute | solution.py:32
  344.2 11.8 %collective-permute-start.5 = (f32[2048,128]{0,1:T(8,128)S(1)}, f32[2048,128]{0,1:T(8,128)S(1)}, u32[]{:S(2)}, u32[]{:S(2)}) collective-permute-start(f32[2048,128]{0,1:T(8,128)S(1)} %fusion.21), channel_id=1, source_target_pairs={{0,32},{32,64},{64,96},{96,128},{128,160},{160,192},{192,224},{224... | collective-permute-start | bytes 3145736 | tf_op jit(solution)/shard_map/while/body/eval_jaxpr/ppermute | solution.py:10
  358.8 9.4 collective-permute-start
  368.3 12.9 %collective-permute-start.1 = (f32[128,1024]{1,0:T(8,128)S(1)}, f32[128,1024]{1,0:T(8,128)S(1)}, u32[]{:S(2)}, u32[]{:S(2)}) collective-permute-start(f32[128,1024]{1,0:T(8,128)S(1)} %add.107), channel_id=1, source_target_pairs={{0,2},{1,3},{2,0},{3,1},{4,6},{5,7},{6,4},{7,5},{8,10},{9,11},{10,... | collective-permute-start | bytes 1572872 | tf_op jit(solution)/shard_map/while/body/eval_jaxpr/ppermute | solution.py:32
  381.2 8.1 collective-permute-start.2
  389.4 14.2 %collective-permute-start.3 = (f32[128,1024]{1,0:T(8,128)S(1)}, f32[128,1024]{1,0:T(8,128)S(1)}, u32[]{:S(2)}, u32[]{:S(2)}) collective-permute-start(f32[128,1024]{1,0:T(8,128)S(1)} %add.109), channel_id=1, source_target_pairs={{0,8},{1,9},{2,10},{3,11},{4,12},{5,13},{6,14},{7,15},{8,0},{9,1},... | collective-permute-start | bytes 1572872 | tf_op jit(solution)/shard_map/while/body/eval_jaxpr/ppermute | solution.py:32
  403.7 22.2 %collective-permute-start.4 = (f32[128,1024]{1,0:T(8,128)S(1)}, f32[128,1024]{1,0:T(8,128)S(1)}, u32[]{:S(2)}, u32[]{:S(2)}) collective-permute-start(f32[128,1024]{1,0:T(8,128)S(1)} %add.110), channel_id=1, source_target_pairs={{0,16},{1,17},{2,18},{3,19},{4,20},{5,21},{6,22},{7,23},{8,24},{9,... | collective-permute-start | bytes 1572872 | tf_op jit(solution)/shard_map/while/body/eval_jaxpr/ppermute | solution.py:32
  434.6 31.4 %collective-permute-start.5 = (f32[2048,128]{0,1:T(8,128)S(1)}, f32[2048,128]{0,1:T(8,128)S(1)}, u32[]{:S(2)}, u32[]{:S(2)}) collective-permute-start(f32[2048,128]{0,1:T(8,128)S(1)} %fusion.21), channel_id=1, source_target_pairs={{0,32},{32,64},{64,96},{96,128},{128,160},{160,192},{192,224},{224... | collective-permute-start | bytes 3145736 | tf_op jit(solution)/shard_map/while/body/eval_jaxpr/ppermute | solution.py:10
  469.0 8.1 collective-permute-start
  477.1 14.4 %collective-permute-start.1 = (f32[128,1024]{1,0:T(8,128)S(1)}, f32[128,1024]{1,0:T(8,128)S(1)}, u32[]{:S(2)}, u32[]{:S(2)}) collective-permute-start(f32[128,1024]{1,0:T(8,128)S(1)} %add.107), channel_id=1, source_target_pairs={{0,2},{1,3},{2,0},{3,1},{4,6},{5,7},{6,4},{7,5},{8,10},{9,11},{10,... | collective-permute-start | bytes 1572872 | tf_op jit(solution)/shard_map/while/body/eval_jaxpr/ppermute | solution.py:32
  491.6 8.4 collective-permute-start.2
  500.0 14.7 %collective-permute-start.3 = (f32[128,1024]{1,0:T(8,128)S(1)}, f32[128,1024]{1,0:T(8,128)S(1)}, u32[]{:S(2)}, u32[]{:S(2)}) collective-permute-start(f32[128,1024]{1,0:T(8,128)S(1)} %add.109), channel_id=1, source_target_pairs={{0,8},{1,9},{2,10},{3,11},{4,12},{5,13},{6,14},{7,15},{8,0},{9,1},... | collective-permute-start | bytes 1572872 | tf_op jit(solution)/shard_map/while/body/eval_jaxpr/ppermute | solution.py:32
  514.8 22.4 %collective-permute-start.4 = (f32[128,1024]{1,0:T(8,128)S(1)}, f32[128,1024]{1,0:T(8,128)S(1)}, u32[]{:S(2)}, u32[]{:S(2)}) collective-permute-start(f32[128,1024]{1,0:T(8,128)S(1)} %add.110), channel_id=1, source_target_pairs={{0,16},{1,17},{2,18},{3,19},{4,20},{5,21},{6,22},{7,23},{8,24},{9,... | collective-permute-start | bytes 1572872 | tf_op jit(solution)/shard_map/while/body/eval_jaxpr/ppermute | solution.py:32
  546.0 41.3 %collective-permute-start.5 = (f32[2048,128]{0,1:T(8,128)S(1)}, f32[2048,128]{0,1:T(8,128)S(1)}, u32[]{:S(2)}, u32[]{:S(2)}) collective-permute-start(f32[2048,128]{0,1:T(8,128)S(1)} %fusion.21), channel_id=1, source_target_pairs={{0,32},{32,64},{64,96},{96,128},{128,160},{160,192},{192,224},{224... | collective-permute-start | bytes 3145736 | tf_op jit(solution)/shard_map/while/body/eval_jaxpr/ppermute | solution.py:10
  590.2 13.9 %collective-permute-start = (f32[128,1024]{1,0:T(8,128)S(1)}, f32[128,1024]{1,0:T(8,128)S(1)}, u32[]{:S(2)}, u32[]{:S(2)}) collective-permute-start(f32[128,1024]{1,0:T(8,128)S(1)} %fusion.20), channel_id=1, source_target_pairs={{0,1},{1,0},{2,3},{3,2},{4,5},{5,4},{6,7},{7,6},{8,9},{9,8},{10,11... | collective-permute-start | bytes 1572872 | tf_op jit(solution)/shard_map/while/body/eval_jaxpr/ppermute | solution.py:32
  604.2 14.7 %collective-permute-start.1 = (f32[128,1024]{1,0:T(8,128)S(1)}, f32[128,1024]{1,0:T(8,128)S(1)}, u32[]{:S(2)}, u32[]{:S(2)}) collective-permute-start(f32[128,1024]{1,0:T(8,128)S(1)} %add.107), channel_id=1, source_target_pairs={{0,2},{1,3},{2,0},{3,1},{4,6},{5,7},{6,4},{7,5},{8,10},{9,11},{10,... | collective-permute-start | bytes 1572872 | tf_op jit(solution)/shard_map/while/body/eval_jaxpr/ppermute | solution.py:32
  619.0 12.3 %collective-permute-start.2 = (f32[128,1024]{1,0:T(8,128)S(1)}, f32[128,1024]{1,0:T(8,128)S(1)}, u32[]{:S(2)}, u32[]{:S(2)}) collective-permute-start(f32[128,1024]{1,0:T(8,128)S(1)} %add.108), channel_id=1, source_target_pairs={{0,4},{1,5},{2,6},{3,7},{4,0},{5,1},{6,2},{7,3},{8,12},{9,13},{10,... | collective-permute-start | bytes 1572872 | tf_op jit(solution)/shard_map/while/body/eval_jaxpr/ppermute | solution.py:32
  631.3 25.5 %collective-permute-start.3 = (f32[128,1024]{1,0:T(8,128)S(1)}, f32[128,1024]{1,0:T(8,128)S(1)}, u32[]{:S(2)}, u32[]{:S(2)}) collective-permute-start(f32[128,1024]{1,0:T(8,128)S(1)} %add.109), channel_id=1, source_target_pairs={{0,8},{1,9},{2,10},{3,11},{4,12},{5,13},{6,14},{7,15},{8,0},{9,1},... | collective-permute-start | bytes 1572872 | tf_op jit(solution)/shard_map/while/body/eval_jaxpr/ppermute | solution.py:32
  656.9 28.9 %collective-permute-start.4 = (f32[128,1024]{1,0:T(8,128)S(1)}, f32[128,1024]{1,0:T(8,128)S(1)}, u32[]{:S(2)}, u32[]{:S(2)}) collective-permute-start(f32[128,1024]{1,0:T(8,128)S(1)} %add.110), channel_id=1, source_target_pairs={{0,16},{1,17},{2,18},{3,19},{4,20},{5,21},{6,22},{7,23},{8,24},{9,... | collective-permute-start | bytes 1572872 | tf_op jit(solution)/shard_map/while/body/eval_jaxpr/ppermute | solution.py:32
  694.5 11.8 %collective-permute-start.5 = (f32[2048,128]{0,1:T(8,128)S(1)}, f32[2048,128]{0,1:T(8,128)S(1)}, u32[]{:S(2)}, u32[]{:S(2)}) collective-permute-start(f32[2048,128]{0,1:T(8,128)S(1)} %fusion.21), channel_id=1, source_target_pairs={{0,32},{32,64},{64,96},{96,128},{128,160},{160,192},{192,224},{224... | collective-permute-start | bytes 3145736 | tf_op jit(solution)/shard_map/while/body/eval_jaxpr/ppermute | solution.py:10
  709.2 9.4 collective-permute-start
  718.6 15.8 %collective-permute-start.1 = (f32[128,1024]{1,0:T(8,128)S(1)}, f32[128,1024]{1,0:T(8,128)S(1)}, u32[]{:S(2)}, u32[]{:S(2)}) collective-permute-start(f32[128,1024]{1,0:T(8,128)S(1)} %add.107), channel_id=1, source_target_pairs={{0,2},{1,3},{2,0},{3,1},{4,6},{5,7},{6,4},{7,5},{8,10},{9,11},{10,... | collective-permute-start | bytes 1572872 | tf_op jit(solution)/shard_map/while/body/eval_jaxpr/ppermute | solution.py:32
  734.5 9.7 %collective-permute-start.2 = (f32[128,1024]{1,0:T(8,128)S(1)}, f32[128,1024]{1,0:T(8,128)S(1)}, u32[]{:S(2)}, u32[]{:S(2)}) collective-permute-start(f32[128,1024]{1,0:T(8,128)S(1)} %add.108), channel_id=1, source_target_pairs={{0,4},{1,5},{2,6},{3,7},{4,0},{5,1},{6,2},{7,3},{8,12},{9,13},{10,... | collective-permute-start | bytes 1572872 | tf_op jit(solution)/shard_map/while/body/eval_jaxpr/ppermute | solution.py:32
  744.3 48.7 %collective-permute-start.3 = (f32[128,1024]{1,0:T(8,128)S(1)}, f32[128,1024]{1,0:T(8,128)S(1)}, u32[]{:S(2)}, u32[]{:S(2)}) collective-permute-start(f32[128,1024]{1,0:T(8,128)S(1)} %add.109), channel_id=1, source_target_pairs={{0,8},{1,9},{2,10},{3,11},{4,12},{5,13},{6,14},{7,15},{8,0},{9,1},... | collective-permute-start | bytes 1572872 | tf_op jit(solution)/shard_map/while/body/eval_jaxpr/ppermute | solution.py:32
  793.1 25.5 %collective-permute-start.4 = (f32[128,1024]{1,0:T(8,128)S(1)}, f32[128,1024]{1,0:T(8,128)S(1)}, u32[]{:S(2)}, u32[]{:S(2)}) collective-permute-start(f32[128,1024]{1,0:T(8,128)S(1)} %add.110), channel_id=1, source_target_pairs={{0,16},{1,17},{2,18},{3,19},{4,20},{5,21},{6,22},{7,23},{8,24},{9,... | collective-permute-start | bytes 1572872 | tf_op jit(solution)/shard_map/while/body/eval_jaxpr/ppermute | solution.py:32
  827.3 11.8 %collective-permute-start.5 = (f32[2048,128]{0,1:T(8,128)S(1)}, f32[2048,128]{0,1:T(8,128)S(1)}, u32[]{:S(2)}, u32[]{:S(2)}) collective-permute-start(f32[2048,128]{0,1:T(8,128)S(1)} %fusion.21), channel_id=1, source_target_pairs={{0,32},{32,64},{64,96},{96,128},{128,160},{160,192},{192,224},{224... | collective-permute-start | bytes 3145736 | tf_op jit(solution)/shard_map/while/body/eval_jaxpr/ppermute | solution.py:10
  842.0 8.1 collective-permute-start
  850.1 12.1 %collective-permute-start.1 = (f32[128,1024]{1,0:T(8,128)S(1)}, f32[128,1024]{1,0:T(8,128)S(1)}, u32[]{:S(2)}, u32[]{:S(2)}) collective-permute-start(f32[128,1024]{1,0:T(8,128)S(1)} %add.107), channel_id=1, source_target_pairs={{0,2},{1,3},{2,0},{3,1},{4,6},{5,7},{6,4},{7,5},{8,10},{9,11},{10,... | collective-permute-start | bytes 1572872 | tf_op jit(solution)/shard_map/while/body/eval_jaxpr/ppermute | solution.py:32
  862.3 8.1 collective-permute-start.2
  870.5 15.0 %collective-permute-start.3 = (f32[128,1024]{1,0:T(8,128)S(1)}, f32[128,1024]{1,0:T(8,128)S(1)}, u32[]{:S(2)}, u32[]{:S(2)}) collective-permute-start(f32[128,1024]{1,0:T(8,128)S(1)} %add.109), channel_id=1, source_target_pairs={{0,8},{1,9},{2,10},{3,11},{4,12},{5,13},{6,14},{7,15},{8,0},{9,1},... | collective-permute-start | bytes 1572872 | tf_op jit(solution)/shard_map/while/body/eval_jaxpr/ppermute | solution.py:32
  885.5 16.7 %collective-permute-start.4 = (f32[128,1024]{1,0:T(8,128)S(1)}, f32[128,1024]{1,0:T(8,128)S(1)}, u32[]{:S(2)}, u32[]{:S(2)}) collective-permute-start(f32[128,1024]{1,0:T(8,128)S(1)} %add.110), channel_id=1, source_target_pairs={{0,16},{1,17},{2,18},{3,19},{4,20},{5,21},{6,22},{7,23},{8,24},{9,... | collective-permute-start | bytes 1572872 | tf_op jit(solution)/shard_map/while/body/eval_jaxpr/ppermute | solution.py:32
  911.0 32.7 %collective-permute-start.5 = (f32[2048,128]{0,1:T(8,128)S(1)}, f32[2048,128]{0,1:T(8,128)S(1)}, u32[]{:S(2)}, u32[]{:S(2)}) collective-permute-start(f32[2048,128]{0,1:T(8,128)S(1)} %fusion.21), channel_id=1, source_target_pairs={{0,32},{32,64},{64,96},{96,128},{128,160},{160,192},{192,224},{224... | collective-permute-start | bytes 3145736 | tf_op jit(solution)/shard_map/while/body/eval_jaxpr/ppermute | solution.py:10
  (8 other events, 234.9 us)
